TPU v7x, 32 devices: a whole 2x2x4 slice. The times are simulated.
32 devices in a mesh: section: 2 (over y), blk: 8 (over z, x), mp: 2 (over core).
Axes of the slice: x: 2, y: 2, z: 4, core: 2. Of those that a mesh axis runs over, the one named last changes fastest.
Arguments:
- queries: bfloat16 [2, 1024, 4096], P('section', 'blk', 'mp'), may hold values from -210 to 210
- encoder_states: bfloat16 [512, 2048], P(('blk', 'section', 'mp')), may hold values from -200 to 200
- norm_gain: float32 [2048], replicated, may hold values from 0.25 to 1.75
- kv_weight: bfloat16 [2, 2048, 2, 512], P('section', 'blk', None, 'mp'), may hold values from -0.125 to 0.125
- span_len: int32 [64], replicated, may hold values from 1 to 57, as said below
- span_owner: int32 [64], replicated, may hold values from 0 to 7, as said below
Outputs:
- attended: bfloat16 [2, 1024, 4096], P('section', 'blk', 'mp')
Inputs may be any that keep to these rules, and one draw needn't show every extreme that they name: `span_owner`: each span lies whole in the slots of one blk index; each blk index owns exactly 8 spans. `span_len`: the spans of one blk index hold at most 64 tokens together, exactly 64 for some blk index in every draw; all spans hold 288 tokens together; one span holds exactly 57 tokens in every draw.
All inputs are finite; a program needn't handle non-finite values.
Results may differ from a plain program's by a relative error of at most 0.0094.
Values may be sent and summed in bfloat16 or wider, within the bound.
No kernel may reach another device: no remote copies, remote signals or barrier semaphores. Data moves between devices by JAX's collectives and lax.ppermute only.
A program may use at most 64 MiB of HBM per device.

v0:
```python
import jax
import jax.numpy as jnp
from jax import lax
from jax.sharding import PartitionSpec as P

HEADS = 32
KVH = 4
HD = 128


def normalize(states, norm_gain):
    widened = states.astype(jnp.float32)
    factor = lax.rsqrt(jnp.mean(widened * widened, axis=-1, keepdims=True) + 1e-05)
    return (widened * factor * norm_gain).astype(jnp.bfloat16)


def slot_loads(span_len, span_owner, block_count):
    owners = span_owner[:, None] == jnp.arange(block_count, dtype=jnp.int32)[None, :]
    return jnp.sum(jnp.where(owners, span_len[:, None], 0), axis=0)


def live_slots(slot_load, row_count, capacity):
    slot_ids = jnp.arange(row_count, dtype=jnp.int32)
    holder = slot_ids // capacity
    picked = holder[:, None] == jnp.arange(slot_load.shape[0], dtype=jnp.int32)[None, :]
    holder_load = jnp.sum(jnp.where(picked, slot_load[None, :], 0), axis=1)
    return slot_ids % capacity < holder_load


def attend_block(state_now, query_grid, key_rows, value_rows, alive):
    running_max, denominator, numerator = state_now
    row_count = key_rows.shape[0]
    groups = query_grid.shape[1]
    head_size = query_grid.shape[3]
    key_grid = key_rows.reshape(row_count, groups, head_size)
    value_grid = value_rows.reshape(row_count, groups, head_size)
    scores = jnp.einsum(
        "qgjd,rgd->qgjr", query_grid, key_grid, preferred_element_type=jnp.float32
    ) * head_size ** (-0.5)
    scores = jnp.where(alive, scores, -1e30)
    new_max = jnp.maximum(running_max, jnp.max(scores, axis=-1))
    weights = jnp.where(alive, jnp.exp(scores - new_max[..., None]), 0.0)
    denominator = jnp.sum(weights, axis=-1)
    numerator = jnp.einsum(
        "qgjr,rgd->qgjd",
        weights.astype(jnp.bfloat16),
        value_grid,
        preferred_element_type=jnp.float32,
    )
    return (new_max, denominator, numerator)


def attend(state_now, query_grid, key_rows, value_rows, slot_load, capacity):
    row_count = key_rows.shape[0]
    alive = live_slots(slot_load, row_count, capacity)
    return attend_block(state_now, query_grid, key_rows, value_rows, alive)


def local(queries, encoder_states, norm_gain, kv_weight, span_len, span_owner):
    gathered = lax.all_gather(encoder_states, ("section", "mp"), axis=0, tiled=True)
    capacity = gathered.shape[0]
    normed = normalize(gathered, norm_gain)
    block_count = lax.axis_size("blk")
    slot_load = slot_loads(span_len, span_owner, block_count)
    group_width = kv_weight.shape[3]
    local_groups = group_width // HD
    group_size = HEADS // KVH
    query_rows = queries.shape[1]
    query_grid = queries[0].reshape(query_rows, local_groups, group_size, HD)
    start_state = (
        jnp.full((query_rows, local_groups, group_size), -1e30, jnp.float32),
        jnp.zeros((query_rows, local_groups, group_size), jnp.float32),
        jnp.zeros((query_rows, local_groups, group_size, HD), jnp.float32),
    )
    projected = jnp.einsum(
        "cr,rtk->ctk",
        normed,
        lax.all_gather(kv_weight, "blk", axis=1, tiled=True)[0],
        preferred_element_type=jnp.float32,
    )
    key_rows = projected[:, 0].astype(jnp.bfloat16)
    value_rows = projected[:, 1].astype(jnp.bfloat16)
    final_state = attend(
        start_state,
        query_grid,
        lax.all_gather(key_rows, "blk", axis=0, tiled=True),
        lax.all_gather(value_rows, "blk", axis=0, tiled=True),
        slot_load,
        capacity,
    )
    denominator = final_state[1]
    numerator = final_state[2]
    attended = (numerator / denominator[..., None]).astype(jnp.bfloat16)
    return attended.reshape(1, query_rows, local_groups * group_size * HD)


def solution(mesh):
    in_specs = (
        P("section", "blk", "mp"),
        P(("blk", "section", "mp"), None),
        P(),
        P("section", "blk", None, "mp"),
        P(),
        P(),
    )
    out_specs = P("section", "blk", "mp")
    return jax.shard_map(local, mesh=mesh, in_specs=in_specs, out_specs=out_specs, check_vma=False)
```

profile of v0, /device:TPU:0, one launch (start us, length us, event | category | flops | bytes accessed | tf_op | source)
XLA Modules:
  0.0 140.6 jit_solution(526181429607966376)
XLA Ops:
  6.5 0.0 all-gather.4.cloned.1.call-start
  6.5 1.7 %copy.13 = bf16[1,256,2,256]{3,1,2,0:T(8,128)(2,1)} copy(bf16[1,256,2,256]{3,2,1,0:T(2,128)(2,1)} %param.9) | data formatting | bytes 524288 | tf_op args[3]
  8.2 0.0 all-gather.4.cloned.1.call-update
  8.2 1.1 copy.25
  9.4 7.5 %all_gather.12 = bf16[64,2048]{1,0:T(8,128)(2,1)S(1)} all-gather(bf16[16,2048]{1,0:T(8,128)(2,1)} %param.7), channel_id=1, replica_groups=mesh['section'=2,'blk'=8,'mp'=2] {'section','mp'}, dimensions={0}, use_global_device_ids=true | all-gather | bytes 327680 | tf_op jit(solution)/shard_map/all_gather | solution.py:60
  16.9 0.8 select_reduce_fusion.1
  17.6 0.1 select_reduce_fusion
  17.7 0.2 fusion.18
  17.9 43.4 %all-gather.4.cloned.1.call-done = bf16[1,2048,2,256]{3,1,2,0:T(8,128)(2,1)} async-done(((bf16[1,256,2,256]{3,1,2,0:T(8,128)(2,1)}), bf16[1,2048,2,256]{3,1,2,0:T(8,128)(2,1)}) %all-gather.4.cloned.1.call-update) | async-done | bytes 2097168 | tf_op jit(solution)/shard_map/all_gather | solution.py:78
  61.3 2.1 %fusion.13 = bf16[64,2,256]{2,0,1:T(8,128)(2,1)S(1)} fusion(bf16[1,2048,2,256]{3,1,2,0:T(8,128)(2,1)} %all-gather.4.cloned.1.call-done, bf16[64,2048]{1,0:T(8,128)(2,1)S(1)} %all_gather.12, f32[2048]{0:T(1024)} %param.8, f32[64]{0:T(128)S(1)} %add_rsqrt_fusion), kind=kOutput, calls=%fused_computation.13 | convolution fusion | flops 134774784 | bytes 2433280 | tf_op jit(solution)/shard_map/cr,rtk->ctk/dot_general | solution.py:75
  63.5 30.8 %all-gather.1 = bf16[512,1,256]{2,0,1:T(8,128)(2,1)S(1)} all-gather(bf16[64,1,256]{2,0,1:T(8,128)(2,1)S(1)} %get-tuple-element.5), channel_id=3, replica_groups=mesh['section'=2,'blk'=8,'mp'=2] {'blk'}, dimensions={0}, use_global_device_ids=true | all-gather | bytes 294912 | tf_op jit(solution)/shard_map/all_gather | solution.py:86
  94.3 0.1 reshape.41
  94.4 2.7 %bitcast_reduce_fusion = (f32[128,2,8]{0,2,1:T(8,128)S(1)}, f32[2,512,128,8]{2,1,3,0:T(8,128)}) fusion(pred[512]{0:T(512)(128)(4,1)S(1)} %fusion.28, bf16[128,2,8,128]{3,2,1,0:T(8,128)(2,1)S(1)} %bitcast.42, bf16[512,2,128,1]{2,1,0,3:T(2,128)(2,1)S(1)} %bitcast.43), kind=kOutput, calls=%fused_computation.1 | convolution fusion | flops 271579136 | bytes 4989440 | tf_op jit(solution)/shard_map/qgjd,rgd->qgjr/dot_general | solution.py:37
  97.1 30.8 %all-gather = bf16[512,1,256]{2,0,1:T(8,128)(2,1)S(1)} all-gather(bf16[64,1,256]{2,0,1:T(8,128)(2,1)S(1)} %get-tuple-element.6), channel_id=2, replica_groups=mesh['section'=2,'blk'=8,'mp'=2] {'blk'}, dimensions={0}, use_global_device_ids=true | all-gather | bytes 294912 | tf_op jit(solution)/shard_map/all_gather | solution.py:87
  127.9 0.1 copy.22
  128.0 0.0 copy-start
  128.0 3.4 %fusion.2 = f32[128,2,8]{0,2,1:T(8,128)S(1)} fusion(f32[2,512,128,8]{2,1,3,0:T(8,128)} %get-tuple-element.8, f32[128,2,8]{0,2,1:T(8,128)S(1)} %broadcast_maximum_fusion, pred[512]{0:T(512)(128)(4,1)S(1)} %fusion.28), kind=kLoop, calls=%fused_computation.5 | loop fusion | flops 5240832 | bytes 4211200 | tf_op jit(solution)/shard_map/reduce_sum | solution.py:43
  131.5 0.0 copy-done
  131.5 1.3 divide_convert_fusion
  132.8 1.0 copy.18
  (5 shorter events, 0.0 us)
Async XLA Ops:
  6.5 54.8 %all-gather.4.cloned.1.call-start = ((), (), s32[]{:S(2)}) async-start(), calls=%async_computation | async-start | bytes 2359296 | tf_op jit(solution)/shard_map/all_gather | solution.py:78
  128.0 3.5 %copy-start = (f32[2,512,128,8]{2,1,3,0:T(8,128)S(1)}, f32[2,512,128,8]{2,1,3,0:T(8,128)}, u32[]{:S(2)}) copy-start(f32[2,512,128,8]{2,1,3,0:T(8,128)} %get-tuple-element.8) | copy-start | bytes 12582916
Sparse Core Ops, SparseCore 0:
  9.5 51.7 all-gather.3
where the time goes:
time: 141 us
  blocking collectives  69.1 us (49%)
  waiting for transfers between devices  43.4 us (31%)
  between operations  13.5 us (10%)
  matrix products  6.14 us (4%)
  other arithmetic  4.49 us (3%)
  local copies, waits for them, and re-layouts  4.05 us (3%)
    all_gather x1, waiting for transfers between devices, local(): lax.all_gather(kv_weight, 'blk', axis=1, tiled=True)[0]  43.4 us
    all_gather x1, blocking collectives, local(): lax.all_gather(key_rows, 'blk', axis=0, tiled=True)  30.8 us
    all_gather x1, blocking collectives, local(): lax.all_gather(value_rows, 'blk', axis=0, tiled=True)  30.8 us
    all_gather x1, blocking collectives, local(): lax.all_gather(encoder_states, ('section', 'mp'), axis=0, tiled=True)  7.46 us
    reduce_sum x1, other arithmetic, attend_block(): denominator = jnp.sum(weights, axis=-1)  3.44 us
    unnamed x4, local copies, waits for them, and re-layouts  2.83 us
  transfers between devices with their start and end apart: 1, of which 1 were waited for; matrix products, arithmetic and copies ran while one was open for 2% of the time, Pallas kernels for 0%

commit v1 on v0

--- a/solution.py
+++ b/solution.py
@@ -6,6 +6,11 @@
 HEADS = 32
 KVH = 4
 HD = 128
+
+
+def swapped_in(value, axis, dim):
+    outgoing = jnp.stack([value] * lax.axis_size(axis))
+    return jnp.concatenate(lax.all_to_all(outgoing, axis, 0, 0), axis=dim)
 
 
 def normalize(states, norm_gain):
@@ -83,7 +88,7 @@
     final_state = attend(
         start_state,
         query_grid,
-        lax.all_gather(key_rows, "blk", axis=0, tiled=True),
+        swapped_in(key_rows, "blk", 0),
         lax.all_gather(value_rows, "blk", axis=0, tiled=True),
         slot_load,
         capacity,

time: 141 us -> 112 us (0.79)
  blocking collectives: 69.1 us -> 39.7 us
  starting transfers between devices: 0.01 us -> 3.41 us
  other arithmetic: 4.49 us -> 2.21 us
  matrix products: 6.14 us -> 4.22 us
    all_gather x1 -> x0, blocking collectives: 30.8 us -> none  [local(): lax.all_gather(key_rows, 'blk', axis=0, tiled=True)]
    all_to_all x0 -> x1, starting transfers between devices: none -> 3.41 us  [swapped_in(): return jnp.concatenate(lax.all_to_all(outgoing, axis, 0, 0), axis=dim)]
    reduce_sum x1, other arithmetic: 3.44 us -> 1.16 us  [attend_block(): denominator = jnp.sum(weights, axis=-1)]
    dot_general x1, matrix products: 2.74 us -> 0.81 us  [attend_block(): jnp.einsum('qgjd,rgd->qgjr', query_grid, key_grid, preferred_element_type...]
    all_gather x1, blocking collectives: 30.8 us -> 32.2 us  [local(): lax.all_gather(value_rows, 'blk', axis=0, tiled=True)]
  transfers between devices with their start and end apart: 1 -> 2, of which waited for: 1 -> 1; matrix products, arithmetic and copies ran while one was open for 2% -> 1% of each run, Pallas kernels for 0% -> 0%
where the time goes in v1:
time: 112 us; the launch traced here: 111 us
  waiting for transfers between devices  44.6 us (40%)
  blocking collectives  39.7 us (35%)
  between operations  13.5 us (12%)
  matrix products  4.22 us (4%)
  local copies, waits for them, and re-layouts  3.79 us (3%)
  starting transfers between devices  3.41 us (3%)
  other arithmetic  2.21 us (2%)
    all_gather x1, waiting for transfers between devices, local(): lax.all_gather(kv_weight, 'blk', axis=1, tiled=True)[0]  44.6 us
    all_gather x1, blocking collectives, local(): lax.all_gather(value_rows, 'blk', axis=0, tiled=True)  32.2 us
    all_gather x1, blocking collectives, local(): lax.all_gather(encoder_states, ('section', 'mp'), axis=0, tiled=True)  7.46 us
    all_to_all x1, starting transfers between devices, swapped_in(): return jnp.concatenate(lax.all_to_all(outgoing, axis, 0, 0), axis=dim)  3.41 us
  transfers between devices with their start and end apart: 2, of which 1 were waited for; matrix products, arithmetic and copies ran while one was open for 1% of the time, Pallas kernels for 0%

profile of v1, /device:TPU:0, one launch (start us, length us, event | category | flops | bytes accessed | tf_op | source)
XLA Modules:
  0.0 111.4 jit_solution(16267699905086506733)
XLA Ops:
  6.5 0.0 copy-start
  6.5 0.0 all-gather.3.cloned.1.call-start
  6.5 1.7 %copy.18 = bf16[1,256,2,256]{3,1,2,0:T(8,128)(2,1)} copy(bf16[1,256,2,256]{3,2,1,0:T(2,128)(2,1)} %param.9) | data formatting | bytes 524288 | tf_op args[3]
  8.3 0.0 all-gather.3.cloned.1.call-update
  8.3 7.5 %all_gather.9 = bf16[64,2048]{1,0:T(8,128)(2,1)S(1)} all-gather(bf16[16,2048]{1,0:T(8,128)(2,1)} %param.7), channel_id=1, replica_groups=mesh['section'=2,'blk'=8,'mp'=2] {'section','mp'}, dimensions={0}, use_global_device_ids=true | all-gather | bytes 327680 | tf_op jit(solution)/shard_map/all_gather | solution.py:65
  15.8 0.8 select_reduce_fusion.1
  16.6 0.2 fusion.18
  16.7 44.6 %all-gather.3.cloned.1.call-done = bf16[1,2048,2,256]{3,1,2,0:T(8,128)(2,1)} async-done(((bf16[1,256,2,256]{3,1,2,0:T(8,128)(2,1)}), bf16[1,2048,2,256]{3,1,2,0:T(8,128)(2,1)}) %all-gather.3.cloned.1.call-update) | async-done | bytes 2097168 | tf_op jit(solution)/shard_map/all_gather | solution.py:83
  61.3 2.1 %fusion.13 = bf16[64,2,256]{2,0,1:T(8,128)(2,1)S(1)} fusion(bf16[1,2048,2,256]{3,1,2,0:T(8,128)(2,1)} %all-gather.3.cloned.1.call-done, bf16[64,2048]{1,0:T(8,128)(2,1)S(1)} %all_gather.9, f32[2048]{0:T(1024)} %param.8, f32[64]{0:T(128)S(1)} %add_rsqrt_fusion), kind=kOutput, calls=%fused_computation.13 | convolution fusion | flops 134774784 | bytes 2433280 | tf_op jit(solution)/shard_map/cr,rtk->ctk/dot_general | solution.py:80
  63.5 0.7 stack.2
  64.2 3.4 %all-to-all-start = ((bf16[8,64,256]{2,1,0:T(8,128)(2,1)}), bf16[8,64,256]{2,1,0:T(8,128)(2,1)S(1)}, u32[]{:S(2)}, u32[]{:S(2)}) async-start(bf16[8,64,256]{2,1,0:T(8,128)(2,1)} %stack.2), calls=%async_computation | async-start | bytes 524288 | tf_op jit(solution)/shard_map/all_to_all | solution.py:13
  67.6 0.0 copy-done
  67.6 0.1 copy.30
  67.8 0.1 select_reduce_fusion
  67.9 32.2 %all-gather = bf16[512,1,256]{2,0,1:T(8,128)(2,1)S(1)} all-gather(bf16[64,1,256]{2,0,1:T(8,128)(2,1)S(1)} %get-tuple-element.6), channel_id=2, replica_groups=mesh['section'=2,'blk'=8,'mp'=2] {'blk'}, dimensions={0}, use_global_device_ids=true | all-gather | bytes 294912 | tf_op jit(solution)/shard_map/all_gather | solution.py:92
  100.1 0.1 copy.27
  100.2 0.0 all-to-all-done
  100.2 0.1 reshape_reshape.3
  100.3 0.8 bitcast_reduce_fusion
  101.1 1.2 %fusion.2 = f32[128,2,8]{0,2,1:T(8,128)S(1)} fusion(f32[2,512,128,8]{2,1,3,0:T(8,128)S(1)} %get-tuple-element.8, f32[128,2,8]{0,2,1:T(8,128)S(1)} %broadcast_maximum_fusion, pred[512]{0:T(512)(128)(4,1)S(1)} %fusion.28), kind=kLoop, calls=%fused_computation.5 | loop fusion | flops 5240832 | bytes 4211200 | tf_op jit(solution)/shard_map/reduce_sum | solution.py:48
  102.3 1.3 %divide_convert_fusion = bf16[128,2,8,128]{0,3,2,1:T(8,128)(2,1)S(1)} fusion(bf16[512,2,128,1]{0,2,3,1:T(8,128)(2,1)S(1)} %bitcast.46, f32[2,512,128,8]{2,1,3,0:T(8,128)S(1)} %get-tuple-element.8, f32[128,2,8]{0,2,1:T(8,128)S(1)} %broadcast_maximum_fusion, pred[512]{0:T(512)(128)(4,1)S(1)} %fusion.28, f32[128,2,8]{0,2,1:T(8,128)S(1)} %fusion.2), kind=kOutput, calls=%fused_computation.14 | convolution fusion | flops 274202624 | bytes 4997632 | tf_op jit(solution)/shard_map/qgjr,rgd->qgjd/dot_general | solution.py:49
  103.6 1.0 copy.23
  (5 shorter events, 0.0 us)
Async XLA Ops:
  6.5 61.1 %copy-start = (bf16[1,128,2048]{2,1,0:T(8,128)(2,1)S(1)}, bf16[1,128,2048]{2,1,0:T(8,128)(2,1)}, u32[]{:S(2)}) copy-start(bf16[1,128,2048]{2,1,0:T(8,128)(2,1)} %param.6) | copy-start | bytes 1572868
  6.5 54.8 %all-gather.3.cloned.1.call-start = ((), (), s32[]{:S(2)}) async-start(), calls=%async_computation.1 | async-start | bytes 2359296 | tf_op jit(solution)/shard_map/all_gather | solution.py:83
  64.2 36.0 %all-to-all-start = ((bf16[8,64,256]{2,1,0:T(8,128)(2,1)}), bf16[8,64,256]{2,1,0:T(8,128)(2,1)S(1)}, u32[]{:S(2)}, u32[]{:S(2)}) async-start(bf16[8,64,256]{2,1,0:T(8,128)(2,1)} %stack.2), calls=%async_computation | async-start | bytes 524288 | tf_op jit(solution)/shard_map/all_to_all | solution.py:13
Sparse Core Ops, SparseCore 0:
  9.5 51.7 all-gather.2
